TPU v7x, 32 devices: a whole 2x2x4 slice. The times are simulated.
32 devices in a mesh: dp: 8 (over y, x, core), expert: 4 (over z).
Axes of the slice: x: 2, y: 2, z: 4, core: 2. Of those that a mesh axis runs over, the one named last changes fastest.
Arguments:
- tokens: bfloat16 [4096, 2048], P(('dp', 'expert')), may hold values from -6 to 6
- routes: int32 [4096, 2], P(('dp', 'expert')), may hold values from 0 to 3, all different within a row; in each aligned block of 128 rows (0 to 127, 128 to 255, ...) at most 80 rows name the same one
- gates: float32 [4096, 2], P(('dp', 'expert')), may hold values from 0.2 to 1
- cotangent: bfloat16 [4096, 2048], P(('dp', 'expert')), may hold values from -6 to 6
- w_gate: bfloat16 [4, 2048, 384], P('expert', 'dp'), may hold values from -0.125 to 0.125
- w_up: bfloat16 [4, 2048, 384], P('expert', 'dp'), may hold values from -0.125 to 0.125
- w_down: bfloat16 [4, 384, 2048], P('expert', None, 'dp'), may hold values from -0.3125 to 0.3125
Outputs:
- mixed: bfloat16 [4096, 2048], P(('dp', 'expert'))
- token_grads: bfloat16 [4096, 2048], P(('dp', 'expert'))
- gate_grads: float32 [4096, 2], P(('dp', 'expert'))
- grad_gate: float32 [4, 2048, 384], P('expert', 'dp')
- grad_up: float32 [4, 2048, 384], P('expert', 'dp')
- grad_down: float32 [4, 384, 2048], P('expert', None, 'dp')
Inputs may be any that keep to these rules, and one draw needn't show every extreme that they name: `routes`: each row names 2 different experts. Within the 128 rows of one device no expert is named by more than 80 rows, a bound that some expert reaches in some device's rows.
All inputs are finite; a program needn't handle non-finite values.
Results may differ from a plain program's by a relative error of at most 0.015.
Values may be sent and summed in bfloat16 or wider, within the bound.
A program may use at most 64 MiB of HBM per device.

v0:
```python
import jax
import jax.numpy as jnp
from jax import lax
from jax.sharding import PartitionSpec as P


def contract_last(left, right):
    return lax.dot_general(
        left, right, (((1,), (1,)), ((), ())), preferred_element_type=jnp.float32
    )


def contract_first(left, right):
    return lax.dot_general(
        left, right, (((0,), (0,)), ((), ())), preferred_element_type=jnp.float32
    )


def body(tokens, routes, gates, cotangent, w_gate, w_up, w_down):
    experts = lax.axis_size("expert")
    token_rows = tokens.shape[0]
    picks = routes.shape[1]
    width = tokens.shape[1]
    capacity = max(2, 5 * token_rows * picks // (4 * experts))
    entries = token_rows * picks
    slot_count = experts * capacity
    flat_routes = routes.reshape(entries)
    member = (flat_routes[:, None] == jnp.arange(experts, dtype=jnp.int32)[None, :]).astype(
        jnp.int32
    )
    earlier = jnp.cumsum(member, axis=0) - member
    target = flat_routes * capacity + jnp.sum(earlier * member, axis=1)
    placing = (jnp.arange(slot_count, dtype=jnp.int32)[:, None] == target[None, :]).astype(
        jnp.bfloat16
    )
    placing_tokens = jnp.sum(placing.reshape(slot_count, token_rows, picks), axis=2)
    outbound = jnp.dot(placing_tokens, tokens, preferred_element_type=jnp.float32).astype(
        jnp.bfloat16
    )
    outbound = outbound.reshape(experts, capacity, width)
    scaled = (gates[:, :, None] * cotangent.astype(jnp.float32)[:, None, :]).astype(jnp.bfloat16)
    grad_outbound = jnp.dot(
        placing, scaled.reshape(entries, width), preferred_element_type=jnp.float32
    )
    grad_outbound = grad_outbound.astype(jnp.bfloat16).reshape(experts, capacity, width)
    inbound = lax.all_to_all(outbound, "expert", split_axis=0, concat_axis=0, tiled=True)
    slot_rows = inbound.reshape(slot_count, width)
    full_gate, full_up, full_down = (
        lax.all_gather(w_gate, "dp", axis=1, tiled=True),
        lax.all_gather(w_up, "dp", axis=1, tiled=True),
        lax.all_gather(w_down, "dp", axis=2, tiled=True),
    )
    full_gate = full_gate[0]
    full_up = full_up[0]
    full_down = full_down[0]
    gate_pre = jnp.dot(slot_rows, full_gate, preferred_element_type=jnp.float32)
    up_pre = jnp.dot(slot_rows, full_up, preferred_element_type=jnp.float32)
    sigma = jax.nn.sigmoid(gate_pre)
    swish = gate_pre * sigma
    hidden = (swish * up_pre).astype(jnp.bfloat16)
    expert_out = jnp.dot(hidden, full_down, preferred_element_type=jnp.float32).astype(jnp.bfloat16)
    returned = lax.all_to_all(
        expert_out.reshape(experts, capacity, width),
        "expert",
        split_axis=0,
        concat_axis=0,
        tiled=True,
    )
    per_entry = contract_first(placing, returned.reshape(slot_count, width)).reshape(
        token_rows, picks, width
    )
    mixed = jnp.sum(gates[:, :, None] * per_entry, axis=1).astype(jnp.bfloat16)
    gate_grads = jnp.sum(cotangent.astype(jnp.float32)[:, None, :] * per_entry, axis=2)
    grad_inbound = lax.all_to_all(grad_outbound, "expert", split_axis=0, concat_axis=0, tiled=True)
    grad_rows = grad_inbound.reshape(slot_count, width)
    d_hidden = contract_last(grad_rows, full_down)
    d_gate = (d_hidden * up_pre * sigma * (1.0 + gate_pre * (1.0 - sigma))).astype(jnp.bfloat16)
    d_up = (d_hidden * swish).astype(jnp.bfloat16)
    part_gate = contract_first(slot_rows, d_gate)
    part_up = contract_first(slot_rows, d_up)
    part_down = contract_first(hidden, grad_rows)
    shares = (
        lax.psum_scatter(
            part_gate.astype(jnp.bfloat16), "dp", scatter_dimension=0, tiled=True
        ).astype(jnp.float32),
        lax.psum_scatter(
            part_up.astype(jnp.bfloat16), "dp", scatter_dimension=0, tiled=True
        ).astype(jnp.float32),
        lax.psum_scatter(
            part_down.astype(jnp.bfloat16), "dp", scatter_dimension=1, tiled=True
        ).astype(jnp.float32),
    )
    entry_grad = (contract_last(d_gate, full_gate) + contract_last(d_up, full_up)).astype(
        jnp.bfloat16
    )
    arrived = lax.all_to_all(
        entry_grad.reshape(experts, capacity, width),
        "expert",
        split_axis=0,
        concat_axis=0,
        tiled=True,
    )
    token_grads = contract_first(placing_tokens, arrived.reshape(slot_count, width)).astype(
        jnp.bfloat16
    )
    return (mixed, token_grads, gate_grads, shares[0][None], shares[1][None], shares[2][None])


def solution(mesh):
    return jax.shard_map(
        body,
        mesh=mesh,
        in_specs=(
            P(("dp", "expert"), None),
            P(("dp", "expert"), None),
            P(("dp", "expert"), None),
            P(("dp", "expert"), None),
            P("expert", "dp", None),
            P("expert", "dp", None),
            P("expert", None, "dp"),
        ),
        out_specs=(
            P(("dp", "expert"), None),
            P(("dp", "expert"), None),
            P(("dp", "expert"), None),
            P("expert", "dp", None),
            P("expert", "dp", None),
            P("expert", None, "dp"),
        ),
        check_vma=False,
    )
```

profile of v0, /device:TPU:13, one launch (start us, length us, event | category | flops | bytes accessed | tf_op | source)
XLA Modules:
  0.0 227.8 jit_solution(18241620535647696961)
XLA Ops:
  13.9 4.9 %all-to-all-start = ((bf16[4,80,2048]{2,1,0:T(8,128)(2,1)}), bf16[4,80,2048]{2,1,0:T(8,128)(2,1)}, u32[]{:S(2)}, u32[]{:S(2)}) async-start(bf16[4,80,2048]{2,1,0:T(8,128)(2,1)} %bitcast.2), calls=%async_computation | async-start | bytes 2621440 | tf_op jit(solution)/shard_map/all_to_all | solution.py:46
  20.6 2.5 %mul.83 = f32[256,2048]{1,0:T(8,128)} reshape(f32[128,2,2048]{2,1,0:T(2,128)S(1)} %mul.82.clone) | data formatting | bytes 4194304 | tf_op jit(solution)/shard_map/mul | solution.py:41
  23.3 3.2 %convolution_convert_fusion.4 = bf16[320,2048]{1,0:T(8,128)(2,1)} fusion(f32[256,2048]{1,0:T(8,128)} %mul.83, f32[256]{0:T(256)S(1)} %mul.80, s32[256]{0:T(256)S(1)} %multiply_add_fusion.1), kind=kOutput, calls=%fused_computation.6 | convolution fusion | flops 337330176 | bytes 3409920 | tf_op jit(solution)/shard_map/dot_general | solution.py:42
  26.6 19.7 %all-to-all-done = bf16[4,80,2048]{2,1,0:T(8,128)(2,1)} async-done(((bf16[4,80,2048]{2,1,0:T(8,128)(2,1)}), bf16[4,80,2048]{2,1,0:T(8,128)(2,1)}, u32[]{:S(2)}, u32[]{:S(2)}) %all-to-all-start) | async-done | bytes 1310752 | tf_op jit(solution)/shard_map/all_to_all | solution.py:46
  46.3 7.0 %all-to-all-start.2 = ((bf16[4,80,2048]{2,1,0:T(8,128)(2,1)}), bf16[4,80,2048]{2,1,0:T(8,128)(2,1)S(1)}, u32[]{:S(2)}, u32[]{:S(2)}) async-start(bf16[4,80,2048]{2,1,0:T(8,128)(2,1)} %bitcast.10), calls=%async_computation.2 | async-start | bytes 2621440 | tf_op jit(solution)/shard_map/all_to_all | solution.py:74
  53.3 2.7 %fusion.9 = f32[320,384]{1,0:T(8,128)S(1)} fusion(bf16[320,2048]{1,0:T(8,128)(2,1)} %bitcast.3, bf16[1,2048,384]{2,1,0:T(8,128)(2,1)} %all-gather.4.cloned.1.call-done), kind=kOutput, calls=%fused_computation.20 | convolution fusion | flops 503316480 | bytes 3375104 | tf_op jit(solution)/shard_map/dot_general | solution.py:56
  56.0 8.4 %all-gather.6.cloned.1.call-done = bf16[1,2048,384]{2,1,0:T(8,128)(2,1)} async-done(((bf16[1,256,384]{2,1,0:T(8,128)(2,1)}), bf16[1,2048,384]{2,1,0:T(8,128)(2,1)}) %all-gather.6.cloned.1.call-update) | async-done | bytes 1572880 | tf_op jit(solution)/shard_map/all_gather | solution.py:50
  64.5 3.4 %fusion.5 = f32[320,384]{1,0:T(8,128)} fusion(bf16[320,2048]{1,0:T(8,128)(2,1)} %bitcast.3, bf16[1,2048,384]{2,1,0:T(8,128)(2,1)} %all-gather.6.cloned.1.call-done), kind=kOutput, calls=%fused_computation.16 | convolution fusion | flops 503316480 | bytes 3375104 | tf_op jit(solution)/shard_map/dot_general | solution.py:57
  67.9 12.5 %all-to-all-done.2 = bf16[4,80,2048]{2,1,0:T(8,128)(2,1)S(1)} async-done(((bf16[4,80,2048]{2,1,0:T(8,128)(2,1)}), bf16[4,80,2048]{2,1,0:T(8,128)(2,1)S(1)}, u32[]{:S(2)}, u32[]{:S(2)}) %all-to-all-start.2) | async-done | bytes 1310752 | tf_op jit(solution)/shard_map/all_to_all | solution.py:74
  80.4 11.6 %all-gather.8.cloned.1.call-done = bf16[1,384,2048]{2,1,0:T(8,128)(2,1)} async-done(((bf16[1,384,256]{2,1,0:T(8,128)(2,1)}), bf16[1,384,2048]{2,1,0:T(8,128)(2,1)}) %all-gather.8.cloned.1.call-update) | async-done | bytes 1572880 | tf_op jit(solution)/shard_map/all_gather | solution.py:51
  92.0 2.5 %multiply_convert_fusion.2 = (bf16[320,384]{1,0:T(8,128)(2,1)S(1)}, bf16[320,384]{1,0:T(8,128)(2,1)S(1)}, bf16[320,384]{1,0:T(8,128)(2,1)S(1)}) fusion(f32[320,384]{1,0:T(8,128)S(1)} %fusion.9, f32[320,384]{1,0:T(8,128)} %fusion.5, bf16[320,2048]{1,0:T(8,128)(2,1)S(1)} %bitcast.72, bf16[1,384,2048]{2,1,0:T(8,128)(2,1)} %all-gather.8.cloned.1.call-done), kind=kOutput, calls=%fused_computation.23 | convolution fusion | flops 505159680 | bytes 4603904 | tf_op jit(solution)/shard_map/dot_general | solution.py:8
  94.4 3.6 %convolution_convert_fusion.2 = bf16[2048,384]{1,0:T(8,128)(2,1)} fusion(bf16[320,2048]{1,0:T(8,128)(2,1)} %bitcast.3, bf16[320,384]{1,0:T(8,128)(2,1)S(1)} %get-tuple-element.9), kind=kOutput, calls=%fused_computation.3 | convolution fusion | flops 504102912 | bytes 3129344 | tf_op jit(solution)/shard_map/dot_general | solution.py:14
  98.1 3.6 %convolution_convert_fusion.1 = bf16[2048,384]{1,0:T(8,128)(2,1)} fusion(bf16[320,2048]{1,0:T(8,128)(2,1)} %bitcast.3, bf16[320,384]{1,0:T(8,128)(2,1)S(1)} %get-tuple-element.8), kind=kOutput, calls=%fused_computation.2 | convolution fusion | flops 504102912 | bytes 3129344 | tf_op jit(solution)/shard_map/dot_general | solution.py:14
  101.8 2.4 %fusion.7 = f32[320,2048]{1,0:T(8,128)S(1)} fusion(bf16[320,384]{1,0:T(8,128)(2,1)S(1)} %get-tuple-element.9, bf16[1,2048,384]{2,1,0:T(8,128)(2,1)} %all-gather.4.cloned.1.call-done), kind=kOutput, calls=%fused_computation.18 | convolution fusion | flops 503316480 | bytes 4440064 | tf_op jit(solution)/shard_map/dot_general | solution.py:8
  104.2 2.0 fusion
  106.2 4.6 %all-to-all-start.3 = ((bf16[4,80,2048]{2,1,0:T(8,128)(2,1)}), bf16[4,80,2048]{2,1,0:T(8,128)(2,1)S(1)}, u32[]{:S(2)}, u32[]{:S(2)}) async-start(bf16[4,80,2048]{2,1,0:T(8,128)(2,1)} %bitcast.75), calls=%async_computation.3 | async-start | bytes 2621440 | tf_op jit(solution)/shard_map/all_to_all | solution.py:96
  110.8 3.4 %convolution_convert_fusion.5 = bf16[320,2048]{1,0:T(8,128)(2,1)} fusion(bf16[320,384]{1,0:T(8,128)(2,1)S(1)} %get-tuple-element.10, bf16[1,384,2048]{2,1,0:T(8,128)(2,1)} %all-gather.8.cloned.1.call-done), kind=kOutput, calls=%fused_computation.7 | convolution fusion | flops 503971840 | bytes 3129344 | tf_op jit(solution)/shard_map/dot_general | solution.py:61
  114.2 24.5 %all-to-all-done.3 = bf16[4,80,2048]{2,1,0:T(8,128)(2,1)S(1)} async-done(((bf16[4,80,2048]{2,1,0:T(8,128)(2,1)}), bf16[4,80,2048]{2,1,0:T(8,128)(2,1)S(1)}, u32[]{:S(2)}, u32[]{:S(2)}) %all-to-all-start.3) | async-done | bytes 1310752 | tf_op jit(solution)/shard_map/all_to_all | solution.py:96
  138.7 7.3 %all-to-all-start.1 = ((bf16[4,80,2048]{2,1,0:T(8,128)(2,1)}), bf16[4,80,2048]{2,1,0:T(8,128)(2,1)}, u32[]{:S(2)}, u32[]{:S(2)}) async-start(bf16[4,80,2048]{2,1,0:T(8,128)(2,1)} %bitcast.7), calls=%async_computation.1 | async-start | bytes 2621440 | tf_op jit(solution)/shard_map/all_to_all | solution.py:62
  146.0 2.2 convolution_convert_fusion
  151.9 21.1 %all-to-all-done.1 = bf16[4,80,2048]{2,1,0:T(8,128)(2,1)} async-done(((bf16[4,80,2048]{2,1,0:T(8,128)(2,1)}), bf16[4,80,2048]{2,1,0:T(8,128)(2,1)}, u32[]{:S(2)}, u32[]{:S(2)}) %all-to-all-start.1) | async-done | bytes 1310752 | tf_op jit(solution)/shard_map/all_to_all | solution.py:62
  173.0 3.1 %multiply_reduce_fusion = (f32[128,2]{0,1:T(2,128)}, bf16[128,2048]{1,0:T(8,128)(2,1)}) fusion(f32[128,2048]{1,0:T(8,128)S(1)} %copy-done.4, f32[128,2]{0,1:T(2,128)S(1)} %copy-done.5, bf16[320,2048,1]{1,0,2:T(8,128)(2,1)} %bitcast.9, pred[128,2,320]{2,1,0:T(4,128)(4,1)S(1)} %eq.68), kind=kOutput, calls=%fused_computation.9 | convolution fusion | flops 337379072 | bytes 2967552 | tf_op jit(solution)/shard_map/dot_general | solution.py:14
  176.2 1.7 bitcast_convert_fusion.2
  179.6 39.7 %reduce-scatter.8.cloned.1.call-done = bf16[384,256]{1,0:T(8,128)(2,1)} async-done(((bf16[384,2048]{1,0:T(8,128)(2,1)}), bf16[384,256]{1,0:T(8,128)(2,1)}) %reduce-scatter.8.cloned.1.call-update) | async-done | bytes 196624 | tf_op jit(solution)/shard_map/reduce_scatter | solution.py:89
  (54 shorter events, 15.9 us)
Async XLA Ops:
  7.2 5.2 %copy-start = (bf16[128,2048]{1,0:T(8,128)(2,1)S(1)}, bf16[128,2048]{1,0:T(8,128)(2,1)}, u32[]{:S(2)}) copy-start(bf16[128,2048]{1,0:T(8,128)(2,1)} %param.7) | copy-start | bytes 1572868
  7.2 46.2 %all-gather.4.cloned.1.call-start = ((), (), s32[]{:S(2)}) async-start(), calls=%async_computation.7 | async-start | bytes 1769472 | tf_op jit(solution)/shard_map/all_gather | solution.py:49
  7.9 56.5 %all-gather.6.cloned.1.call-start = ((), (), s32[]{:S(2)}) async-start(), calls=%async_computation.8 | async-start | bytes 1769472 | tf_op jit(solution)/shard_map/all_gather | solution.py:50
  13.9 5.6 %copy-start.1 = (bf16[128,2048]{1,0:T(8,128)(2,1)S(1)}, bf16[128,2048]{1,0:T(8,128)(2,1)}, u32[]{:S(2)}) copy-start(bf16[128,2048]{1,0:T(8,128)(2,1)} %param.10) | copy-start | bytes 1572868
  13.9 32.4 %all-to-all-start = ((bf16[4,80,2048]{2,1,0:T(8,128)(2,1)}), bf16[4,80,2048]{2,1,0:T(8,128)(2,1)}, u32[]{:S(2)}, u32[]{:S(2)}) async-start(bf16[4,80,2048]{2,1,0:T(8,128)(2,1)} %bitcast.2), calls=%async_computation | async-start | bytes 2621440 | tf_op jit(solution)/shard_map/all_to_all | solution.py:46
  18.8 73.2 %all-gather.8.cloned.1.call-start = ((), (), s32[]{:S(2)}) async-start(), calls=%async_computation.9 | async-start | bytes 1769472 | tf_op jit(solution)/shard_map/all_gather | solution.py:51
  20.6 2.5 %copy-start.5 = (f32[128,2]{0,1:T(2,128)S(1)}, f32[128,2]{0,1:T(2,128)}, u32[]{:S(2)}) copy-start(f32[128,2]{0,1:T(2,128)} %param.9) | copy-start | bytes 3076
  46.3 34.1 %all-to-all-start.2 = ((bf16[4,80,2048]{2,1,0:T(8,128)(2,1)}), bf16[4,80,2048]{2,1,0:T(8,128)(2,1)S(1)}, u32[]{:S(2)}, u32[]{:S(2)}) async-start(bf16[4,80,2048]{2,1,0:T(8,128)(2,1)} %bitcast.10), calls=%async_computation.2 | async-start | bytes 2621440 | tf_op jit(solution)/shard_map/all_to_all | solution.py:74
  53.3 122.8 %reduce-scatter.4.cloned.1.call-start = ((), (), s32[]{:S(2)}) async-start(), calls=%async_computation.10 | async-start | bytes 1769472 | tf_op jit(solution)/shard_map/reduce_scatter | solution.py:83
  98.1 79.8 %reduce-scatter.6.cloned.1.call-start = ((), (), s32[]{:S(2)}) async-start(), calls=%async_computation.11 | async-start | bytes 1769472 | tf_op jit(solution)/shard_map/reduce_scatter | solution.py:86
  101.8 2.4 %copy-start.3 = (bf16[1,2048,384]{2,1,0:T(8,128)(2,1)S(1)}, bf16[1,2048,384]{2,1,0:T(8,128)(2,1)}, u32[]{:S(2)}) copy-start(bf16[1,2048,384]{2,1,0:T(8,128)(2,1)} %all-gather.6.cloned.1.call-done) | copy-start | bytes 4718596
  106.2 32.5 %all-to-all-start.3 = ((bf16[4,80,2048]{2,1,0:T(8,128)(2,1)}), bf16[4,80,2048]{2,1,0:T(8,128)(2,1)S(1)}, u32[]{:S(2)}, u32[]{:S(2)}) async-start(bf16[4,80,2048]{2,1,0:T(8,128)(2,1)} %bitcast.75), calls=%async_computation.3 | async-start | bytes 2621440 | tf_op jit(solution)/shard_map/all_to_all | solution.py:96
  138.7 34.3 %all-to-all-start.1 = ((bf16[4,80,2048]{2,1,0:T(8,128)(2,1)}), bf16[4,80,2048]{2,1,0:T(8,128)(2,1)}, u32[]{:S(2)}, u32[]{:S(2)}) async-start(bf16[4,80,2048]{2,1,0:T(8,128)(2,1)} %bitcast.7), calls=%async_computation.1 | async-start | bytes 2621440 | tf_op jit(solution)/shard_map/all_to_all | solution.py:62
  146.0 73.3 %reduce-scatter.8.cloned.1.call-start = ((), (), s32[]{:S(2)}) async-start(), calls=%async_computation.12 | async-start | bytes 1769472 | tf_op jit(solution)/shard_map/reduce_scatter | solution.py:89
  148.2 1.1 copy-start.2
  150.4 22.6 %copy-start.4 = (f32[128,2048]{1,0:T(8,128)S(1)}, f32[128,2048]{1,0:T(8,128)}, u32[]{:S(2)}) copy-start(f32[128,2048]{1,0:T(8,128)} %convert_element_type.67) | copy-start | bytes 3145732
Sparse Core Ops, SparseCore 0:
  9.9 27.0 all-gather.3
  38.9 25.5 all-gather.5
  66.3 25.5 all-gather.7
  98.2 37.9 reduce-scatter.3
  139.3 38.3 reduce-scatter.5
  180.9 38.3 reduce-scatter.7
where the time goes:
time: 230 us; the launch traced here: 228 us
  waiting for transfers between devices  140 us (61%)
  matrix products  35 us (15%)
  starting transfers between devices  23.9 us (10%)
  between operations  14.2 us (6%)
  other arithmetic  8.5 us (4%)
  local copies, waits for them, and re-layouts  6.48 us (3%)
    reduce_scatter x1, waiting for transfers between devices, body(): lax.psum_scatter(part_down.astype(jnp.bfloat16), 'dp', scatter_dimension=...  39.7 us
    all_to_all x1, waiting for transfers between devices, body(): lax.all_to_all(entry_grad.reshape(experts, capacity, width), 'expert', sp...  24.5 us
    all_to_all x1, waiting for transfers between devices, body(): lax.all_to_all(expert_out.reshape(experts, capacity, width), 'expert', sp...  21.1 us
    all_to_all x1, waiting for transfers between devices, body(): lax.all_to_all(outbound, 'expert', split_axis=0, concat_axis=0, tiled=True)  19.7 us
    dot_general x5, matrix products, contract_first(): lax.dot_general(left, right, (((0,), (0,)), ((), ())), preferred_element_...  13.9 us
    all_to_all x1, waiting for transfers between devices, body(): lax.all_to_all(grad_outbound, 'expert', split_axis=0, concat_axis=0, tile...  12.5 us
    all_gather x1, waiting for transfers between devices, body(): lax.all_gather(w_down, 'dp', axis=2, tiled=True)  11.6 us
    all_gather x1, waiting for transfers between devices, body(): lax.all_gather(w_up, 'dp', axis=1, tiled=True)  8.45 us
  transfers between devices with their start and end apart: 10, of which 7 were waited for; matrix products, arithmetic and copies ran while one was open for 18% of the time, Pallas kernels for 0%

commit v1 on v0

v1 whole, which is shorter than its diff:
```python
import functools

import jax
import jax.numpy as jnp
from jax import lax
from jax.experimental import pallas as pl
from jax.experimental.pallas import tpu as pltpu
from jax.sharding import PartitionSpec as P

F32 = jnp.float32
BF16 = jnp.bfloat16


def dot(left, right, dims):
    return lax.dot_general(left, right, (dims, ((), ())), preferred_element_type=F32)


def kernel(
    experts, groups, cap,
    tokens_ref, cot_ref, gates_ref, gates_t_ref, routes_t_ref, w_ref,
    mixed_ref, token_grads_ref, gate_grads_ref, share_ref,
    place_ref, pick_ref, x_out, x_in, g_out, g_in, y_out, y_in, e_out, e_in,
    weights, gate_pre_ref, up_pre_ref, hidden_ref, d_gate_ref, d_up_ref,
    part, pair_in, summed, rs_in,
    a2a_send, a2a_recv, ag_send, fwd_send, ag_recv, pair_send, pair_recv, rs_send, rs_recv,
):
    me = lax.axis_index("expert")
    here = lax.axis_index("dp")
    chips = groups // 2
    chip = here // 2
    core = here % 2
    partner = here + 1 - 2 * core
    rows = tokens_ref.shape[0]
    width = tokens_ref.shape[1]
    shard = w_ref.shape[1]
    slots = experts * cap

    hops = sorted(range(1, experts), key=lambda s: (abs(2 * s - experts), s))
    chip_hops = sorted(range(1, chips), key=lambda s: (abs(2 * s - chips), s))

    barrier = pltpu.get_barrier_semaphore()
    for s in hops:
        pl.semaphore_signal(barrier, inc=1, device_id={"expert": (me + s) % experts})
    for s in chip_hops:
        pl.semaphore_signal(barrier, inc=1, device_id={"dp": (chip + s) % chips * 2 + core})
    pl.semaphore_signal(barrier, inc=1, device_id={"dp": partner})
    pl.semaphore_wait(barrier, len(hops) + len(chip_hops) + 1)

    def shard_of(ref, owner):
        return ref.at[:, pl.ds(pl.multiple_of(owner * shard, shard), shard), :]

    def weight_send(target, sem):
        return pltpu.make_async_remote_copy(
            src_ref=w_ref, dst_ref=shard_of(weights, here),
            send_sem=ag_send.at[sem], recv_sem=ag_recv.at[here],
            device_id={"dp": target},
        )

    def weight_forward(s):
        source = (chip + s) % chips * 2 + core
        return pltpu.make_async_remote_copy(
            src_ref=shard_of(weights, source), dst_ref=shard_of(weights, source),
            send_sem=fwd_send.at[s], recv_sem=ag_recv.at[source],
            device_id={"dp": partner},
        )

    def weight_arrival(source):
        return pltpu.make_async_remote_copy(
            src_ref=w_ref, dst_ref=shard_of(weights, source),
            send_sem=ag_send.at[0], recv_sem=ag_recv.at[source],
            device_id={"dp": partner},
        )

    for s in chip_hops:
        weight_send((chip + s) % chips * 2 + core, s).start()
    weight_send(partner, 0).start()

    def exchange(number, out, into, s):
        target = (me + s) % experts
        return pltpu.make_async_remote_copy(
            src_ref=out.at[target], dst_ref=into.at[me],
            send_sem=a2a_send.at[number, s], recv_sem=a2a_recv.at[number, me],
            device_id={"expert": target},
        )

    def arrival(number, out, into, s):
        source = (me + s) % experts
        return pltpu.make_async_remote_copy(
            src_ref=out.at[source], dst_ref=into.at[source],
            send_sem=a2a_send.at[number, s], recv_sem=a2a_recv.at[number, source],
            device_id={"expert": source},
        )

    routes_t = routes_t_ref[...]
    expert_ids = lax.broadcasted_iota(jnp.int32, (experts, rows), 0)
    first = expert_ids == routes_t[0:1]
    second = expert_ids == routes_t[1:2]
    member = jnp.where(first | second, 1.0, 0.0)
    earlier = jnp.where(
        lax.broadcasted_iota(jnp.int32, (rows, rows), 0)
        < lax.broadcasted_iota(jnp.int32, (rows, rows), 1), 1.0, 0.0)
    rank = dot(member.astype(BF16), earlier.astype(BF16), ((1,), (0,)))
    places = lax.broadcasted_iota(jnp.int32, (cap, rows), 0)
    for e in range(experts):
        hit = (rank[e:e + 1].astype(jnp.int32) == places).astype(F32)
        for k in range(2):
            named = (routes_t[k:k + 1] == e).astype(F32)
            pick_ref[e * cap:(e + 1) * cap, k * rows:(k + 1) * rows] = (hit * named).astype(BF16)
        place_ref[e] = (hit * member[e:e + 1]).astype(BF16)

    for s in hops + [0]:
        target = (me + s) % experts
        x_out[target] = dot(place_ref[target], tokens_ref[...], ((1,), (0,))).astype(BF16)
        if s:
            exchange(0, x_out, x_in, s).start()
        else:
            x_in[me] = x_out[me]
    for s in hops + [0]:
        target = (me + s) % experts
        at = pl.ds(pl.multiple_of(target * cap, cap), cap)
        gate = jnp.sum(
            pick_ref[at, 0:rows].astype(F32) * gates_t_ref[0:1]
            + pick_ref[at, rows:2 * rows].astype(F32) * gates_t_ref[1:2],
            axis=1, keepdims=True)
        g_out[target] = (
            gate * dot(place_ref[target], cot_ref[...], ((1,), (0,)))).astype(BF16)
        if s:
            exchange(1, g_out, g_in, s).start()
        else:
            g_in[me] = g_out[me]

    weights[:, pl.ds(pl.multiple_of(here * shard, shard), shard), :] = w_ref[...]
    for s in reversed(chip_hops):
        weight_arrival((chip + s) % chips * 2 + core).wait_recv()
        weight_forward(s).start()
    weight_arrival(partner).wait_recv()
    for s in reversed(chip_hops):
        weight_arrival((chip + s) % chips * 2 + 1 - core).wait_recv()
    for s in hops:
        arrival(0, x_out, x_in, s).wait_recv()

    steps = 2
    per = experts // steps
    tall = per * cap

    @pl.loop(0, steps)
    def _(i):
        at = pl.ds(pl.multiple_of(i * tall, tall), tall)
        x = x_in[pl.ds(i * per, per)].reshape(tall, width)
        gate_pre = dot(x, weights[0], ((1,), (0,)))
        up_pre = dot(x, weights[1], ((1,), (0,)))
        gate_pre_ref[at, :] = gate_pre
        up_pre_ref[at, :] = up_pre
        hidden = (gate_pre * jax.nn.sigmoid(gate_pre) * up_pre).astype(BF16)
        hidden_ref[at, :] = hidden
        y_out[pl.ds(i * per, per)] = dot(hidden, weights[2], ((1,), (1,))).astype(BF16).reshape(
            per, cap, width)

    for s in hops:
        exchange(2, y_out, y_in, s).start()
    y_in[me] = y_out[me]

    for s in hops:
        arrival(1, g_out, g_in, s).wait_recv()

    @pl.loop(0, steps)
    def _(i):
        at = pl.ds(pl.multiple_of(i * tall, tall), tall)
        g = g_in[pl.ds(i * per, per)].reshape(tall, width)
        d_hidden = dot(g, weights[2], ((1,), (0,)))
        gate_pre = gate_pre_ref[at, :]
        up_pre = up_pre_ref[at, :]
        sigma = jax.nn.sigmoid(gate_pre)
        d_gate = (d_hidden * up_pre * sigma * (1.0 + gate_pre * (1.0 - sigma))).astype(BF16)
        d_up = (d_hidden * (gate_pre * sigma)).astype(BF16)
        d_gate_ref[at, :] = d_gate
        d_up_ref[at, :] = d_up
        entry = dot(d_gate, weights[0], ((1,), (1,))) + dot(d_up, weights[1], ((1,), (1,)))
        e_out[pl.ds(i * per, per)] = entry.astype(BF16).reshape(per, cap, width)

    for s in hops:
        exchange(3, e_out, e_in, s).start()
    e_in[me] = e_out[me]

    piece = 256

    @pl.loop(0, width // piece)
    def _(i):
        at = pl.ds(pl.multiple_of(i * piece, piece), piece)
        x = x_in[:, :, at].reshape(slots, piece)
        part[0, at, :] = dot(x, d_gate_ref[...], ((0,), (0,))).astype(BF16)
        part[1, at, :] = dot(x, d_up_ref[...], ((0,), (0,))).astype(BF16)
        g = g_in[:, :, at].reshape(slots, piece)
        part[2, at, :] = dot(g, hidden_ref[...], ((0,), (0,))).astype(BF16)

    def pair_send_of(s):
        target = (chip + s) % chips
        return pltpu.make_async_remote_copy(
            src_ref=shard_of(part, target * 2 + 1 - core), dst_ref=pair_in.at[s],
            send_sem=pair_send.at[s], recv_sem=pair_recv.at[s],
            device_id={"dp": partner},
        )

    def share_send_of(s):
        target = (chip + s) % chips
        return pltpu.make_async_remote_copy(
            src_ref=summed.at[s], dst_ref=rs_in.at[s],
            send_sem=rs_send.at[s], recv_sem=rs_recv.at[s],
            device_id={"dp": target * 2 + core},
        )

    def own_sum(s):
        owner = (chip + s) % chips * 2 + core
        own = part[:, pl.ds(pl.multiple_of(owner * shard, shard), shard), :]
        return own.astype(F32) + pair_in[s].astype(F32)

    for s in chip_hops + [0]:
        pair_send_of(s).start()
    for s in chip_hops:
        pair_send_of(s).wait_recv()
        summed[s] = own_sum(s).astype(BF16)
        share_send_of(s).start()
    pair_send_of(0).wait_recv()
    share_ref[...] = own_sum(0)
    for s in reversed(chip_hops):
        share_send_of(s).wait_recv()
        share_ref[...] += rs_in[s].astype(F32)

    for s in hops:
        arrival(2, y_out, y_in, s).wait_recv()

    @pl.loop(0, width // piece)
    def _(i):
        at = pl.ds(pl.multiple_of(i * piece, piece), piece)
        y = y_in[:, :, at].reshape(slots, piece)
        per_entry = dot(pick_ref[...], y, ((0,), (0,)))
        head, tail = per_entry[:rows], per_entry[rows:]
        mixed_ref[:, at] = (
            gates_ref[:, 0:1] * head + gates_ref[:, 1:2] * tail).astype(BF16)
        cot = cot_ref[:, at].astype(F32)
        sums = jnp.concatenate(
            [jnp.sum(cot * head, axis=1, keepdims=True),
             jnp.sum(cot * tail, axis=1, keepdims=True)], axis=1)
        gate_grads_ref[...] = jnp.where(i == 0, 0.0, gate_grads_ref[...]) + sums

    for s in hops:
        arrival(3, e_out, e_in, s).wait_recv()

    @pl.loop(0, width // piece)
    def _(i):
        at = pl.ds(pl.multiple_of(i * piece, piece), piece)
        y = e_in[:, :, at].reshape(slots, piece)
        per_entry = dot(pick_ref[...], y, ((0,), (0,)))
        token_grads_ref[:, at] = (per_entry[:rows] + per_entry[rows:]).astype(BF16)

    for s in chip_hops:
        weight_send((chip + s) % chips * 2 + core, s).wait_send()
        weight_forward(s).wait_send()
        pair_send_of(s).wait_send()
        share_send_of(s).wait_send()
    weight_send(partner, 0).wait_send()
    pair_send_of(0).wait_send()
    for s in hops:
        exchange(0, x_out, x_in, s).wait_send()
        exchange(1, g_out, g_in, s).wait_send()
        exchange(2, y_out, y_in, s).wait_send()
        exchange(3, e_out, e_in, s).wait_send()


def body(tokens, routes, gates, cotangent, w_gate, w_up, w_down):
    experts = lax.axis_size("expert")
    groups = lax.axis_size("dp")
    rows, width = tokens.shape
    picks = routes.shape[1]
    hidden = w_gate.shape[2]
    shard = w_gate.shape[1]
    cap = max(2, 5 * rows * picks // (4 * experts))
    cap = -(-cap // 16) * 16
    slots = experts * cap
    chips = groups // 2
    stacked = jnp.stack([w_gate[0], w_up[0], w_down[0].T])
    vmem = pl.BlockSpec(memory_space=pltpu.VMEM)
    dma = pltpu.SemaphoreType.DMA
    block = pltpu.VMEM((experts, cap, width), BF16)
    mixed, token_grads, gate_grads, share = pl.pallas_call(
        functools.partial(kernel, experts, groups, cap),
        out_shape=(
            jax.ShapeDtypeStruct((rows, width), BF16),
            jax.ShapeDtypeStruct((rows, width), BF16),
            jax.ShapeDtypeStruct((rows, picks), F32),
            jax.ShapeDtypeStruct((3, shard, hidden), F32),
        ),
        in_specs=[vmem] * 6,
        out_specs=(vmem,) * 4,
        scratch_shapes=[
            pltpu.VMEM((experts, cap, rows), BF16),
            pltpu.VMEM((slots, picks * rows), BF16),
            *([block] * 8),
            pltpu.VMEM((3, width, hidden), BF16),
            pltpu.VMEM((slots, hidden), F32),
            pltpu.VMEM((slots, hidden), F32),
            pltpu.VMEM((slots, hidden), BF16),
            pltpu.VMEM((slots, hidden), BF16),
            pltpu.VMEM((slots, hidden), BF16),
            pltpu.VMEM((3, width, hidden), BF16),
            pltpu.VMEM((chips, 3, shard, hidden), BF16),
            pltpu.VMEM((chips, 3, shard, hidden), BF16),
            pltpu.VMEM((chips, 3, shard, hidden), BF16),
            dma((4, experts)), dma((4, experts)),
            dma((chips,)), dma((chips,)), dma((groups,)),
            dma((chips,)), dma((chips,)), dma((chips,)), dma((chips,)),
        ],
        compiler_params=pltpu.CompilerParams(
            collective_id=0, has_side_effects=True, vmem_limit_bytes=58 * 1024 * 1024
        ),
        name="routed_experts",
    )(tokens, cotangent, gates, gates.T, routes.T, stacked)
    return (mixed, token_grads, gate_grads, share[0][None], share[1][None], share[2].T[None])


def solution(mesh):
    return jax.shard_map(
        body,
        mesh=mesh,
        in_specs=(
            P(("dp", "expert"), None),
            P(("dp", "expert"), None),
            P(("dp", "expert"), None),
            P(("dp", "expert"), None),
            P("expert", "dp", None),
            P("expert", "dp", None),
            P("expert", None, "dp"),
        ),
        out_specs=(
            P(("dp", "expert"), None),
            P(("dp", "expert"), None),
            P(("dp", "expert"), None),
            P("expert", "dp", None),
            P("expert", "dp", None),
            P("expert", None, "dp"),
        ),
        check_vma=False,
    )
```

time: 230 us -> 147 us (0.64)
  waiting for transfers between devices: 140 us -> 0 us
  Pallas kernels: 0 us -> 135 us
  matrix products: 35 us -> 0 us
  starting transfers between devices: 23.9 us -> 0 us
  between operations: 14.2 us -> 0.65 us
  other arithmetic: 8.5 us -> 1.96 us
    pallas_call x0 -> x1, Pallas kernels: none -> 135 us  [body(): pl.pallas_call(functools.partial(kernel, experts, groups, cap), out_shape...]
    all_to_all x4 -> x0, waiting for transfers between devices: 77.9 us -> none  [the longest x1 24.5 us: body(): lax.all_to_all(entry_grad.reshape(experts, capacity, width), 'expert', sp...]
    reduce_scatter x3 -> x0, waiting for transfers between devices: 39.7 us -> none  [the longest x1 39.7 us: body(): lax.psum_scatter(part_down.astype(jnp.bfloat16), 'dp', scatter_dimension=...]
    dot_general x13 -> x0, matrix products: 35 us -> none  [the longest x5 13.9 us: contract_first(): lax.dot_general(left, right, (((0,), (0,)), ((), ())), preferred_element_...]
    all_to_all x4 -> x0, starting transfers between devices: 23.8 us -> none  [the longest x1 7.28 us: body(): lax.all_to_all(expert_out.reshape(experts, capacity, width), 'expert', sp...]
    all_gather x3 -> x0, waiting for transfers between devices: 20 us -> none  [the longest x1 11.6 us: body(): lax.all_gather(w_down, 'dp', axis=2, tiled=True)]
    broadcast_in_dim x3 -> x0, other arithmetic: 5.1 us -> none  [the longest x1 1.7 us: body(): shares[0][None]]
    unnamed x14 -> x10, local copies, waits for them, and re-layouts: 1.96 us -> 6.49 us
  transfers between devices with their start and end apart: 10 -> 0, of which waited for: 7 -> 0; matrix products, arithmetic and copies ran while one was open for 18% -> 0% of each run, Pallas kernels for 0% -> 0%
where the time goes in v1:
time: 147 us
  Pallas kernels  135 us (92%)
  local copies, waits for them, and re-layouts  8.73 us (6%)
  other arithmetic  1.96 us (1%)
    pallas_call x1, Pallas kernels, body(): pl.pallas_call(functools.partial(kernel, experts, groups, cap), out_shape...  135 us
    unnamed x10, local copies, waits for them, and re-layouts  6.49 us

profile of v1, /device:TPU:13, one launch (start us, length us, event | category | flops | bytes accessed | tf_op | source)
XLA Modules:
  0.0 146.6 jit_solution(11797169808761163002)
XLA Ops:
  0.6 1.4 copy.14.gates_ref
  2.0 1.1 copy.13
  3.1 2.0 %pad_maximum_fusion.w_ref = bf16[3,256,384]{2,1,0:T(8,128)(2,1)} fusion(bf16[1,256,384]{2,1,0:T(8,128)(2,1)S(1)} %bitcast.13, bf16[1,256,384]{2,1,0:T(8,128)(2,1)} %param.12, bf16[1,256,384]{2,1,0:T(8,128)(2,1)} %param.11), kind=kLoop, calls=%fused_computation | loop fusion | flops 589824 | bytes 1179648 | tf_op jit(solution)/shard_map/stack | solution.py:281
  5.1 135.3 %routed_experts.1 = (bf16[128,2048]{1,0:T(8,128)(2,1)}, bf16[128,2048]{1,0:T(8,128)(2,1)}, f32[128,2]{1,0:T(8,128)}, f32[3,256,384]{2,1,0:T(8,128)}) custom-call(bf16[128,2048]{1,0:T(8,128)(2,1)} %tokens_ref.1, bf16[128,2048]{1,0:T(8,128)(2,1)} %cot_ref.1, f32[128,2]{1,0:T(8,128)} %copy.14.gates_ref, f32[2,128]{1,0:T(2,128)} %bitcast.14, s32[2,128]{1,0:T(2,128)} %bitcast.15, ...), custom_call_target="tpu_custom_call" | custom-call | tf_op jit(solution)/shard_map/routed_experts/pallas_call | solution.py:285
  140.4 1.5 %copy.15 = f32[128,2]{0,1:T(2,128)} copy(f32[128,2]{1,0:T(8,128)} %get-tuple-element.16) | data formatting | bytes 2048
  141.9 0.0 copy-start.1
  141.9 2.2 %slice_bitcast_fusion = (f32[1,384,256]{1,2,0:T(8,128)S(1)}, f32[1,256,384]{2,1,0:T(8,128)}, f32[1,256,384]{2,1,0:T(8,128)}) fusion(f32[3,256,384]{2,1,0:T(8,128)} %get-tuple-element.13), kind=kLoop, calls=%fused_computation.1 | loop fusion | bytes 2359296 | tf_op jit(solution)/shard_map/broadcast_in_dim | solution.py:318
  144.1 0.0 copy-start
  144.1 0.9 copy.16
  145.0 0.0 copy-done.1
  145.0 0.8 copy.19
  145.8 0.0 copy-done
  145.8 0.8 copy.20
Async XLA Ops:
  141.9 3.2 %copy-start.1 = (bf16[128,2048]{1,0:T(8,128)(2,1)S(1)}, bf16[128,2048]{1,0:T(8,128)(2,1)}, u32[]{:S(2)}) copy-start(bf16[128,2048]{1,0:T(8,128)(2,1)} %get-tuple-element.29) | copy-start | bytes 1572868
  144.1 1.7 %copy-start = (bf16[128,2048]{1,0:T(8,128)(2,1)S(1)}, bf16[128,2048]{1,0:T(8,128)(2,1)}, u32[]{:S(2)}) copy-start(bf16[128,2048]{1,0:T(8,128)(2,1)} %get-tuple-element.30) | copy-start | bytes 1572868

commit v2 on v1

--- a/solution.py
+++ b/solution.py
@@ -15,7 +15,7 @@
     return lax.dot_general(left, right, (dims, ((), ())), preferred_element_type=F32)
 
 
-def kernel(
+def direct_kernel(
     experts, groups, cap,
     tokens_ref, cot_ref, gates_ref, gates_t_ref, routes_t_ref, w_ref,
     mixed_ref, token_grads_ref, gate_grads_ref, share_ref,
@@ -267,7 +267,7 @@
         exchange(3, e_out, e_in, s).wait_send()
 
 
-def body(tokens, routes, gates, cotangent, w_gate, w_up, w_down):
+def direct_body(tokens, routes, gates, cotangent, w_gate, w_up, w_down):
     experts = lax.axis_size("expert")
     groups = lax.axis_size("dp")
     rows, width = tokens.shape
@@ -283,7 +283,7 @@
     dma = pltpu.SemaphoreType.DMA
     block = pltpu.VMEM((experts, cap, width), BF16)
     mixed, token_grads, gate_grads, share = pl.pallas_call(
-        functools.partial(kernel, experts, groups, cap),
+        functools.partial(direct_kernel, experts, groups, cap),
         out_shape=(
             jax.ShapeDtypeStruct((rows, width), BF16),
             jax.ShapeDtypeStruct((rows, width), BF16),
@@ -318,6 +318,502 @@
     return (mixed, token_grads, gate_grads, share[0][None], share[1][None], share[2].T[None])
 
 
+def relay_kernel(
+    cap,
+    tokens_ref, cot_ref, gates_ref, meta_ref, wg_ref, wu_ref, wd_ref,
+    mixed_ref, token_grads_ref, gate_grads_ref, share_g_ref, share_u_ref, share_d_ref,
+    pick_ref, relay_pick, meta_in, raw_x, raw_g, x_buddy, g_buddy, x_fw, g_fw, x_in, g_in,
+    y_out, e_out, y_near, e_near, y_far, e_far, y_part, e_part, y_mix, e_mix, gg_out, gg_in,
+    weights, gate_pre_ref, up_pre_ref, hidden_ref, d_gate_ref, d_up_ref,
+    part, pair_in, summed, rs_in,
+    raw_send, raw_recv, meta_send, meta_recv, near_send, near_recv, fw_send, fw_recv,
+    far_send, far_recv, mix_send, mix_recv, gg_send, gg_recv,
+    ag_send, fwd_send, ag_recv, pair_send, pair_recv, rs_send, rs_recv,
+):
+    experts = 4
+    me = lax.axis_index("expert")
+    here = lax.axis_index("dp")
+    chips = pair_in.shape[0]
+    chip = here // 2
+    core = here % 2
+    partner = here + 1 - 2 * core
+    rows = tokens_ref.shape[0]
+    width = tokens_ref.shape[1]
+    shard = wg_ref.shape[0]
+    slots = experts * cap
+    half = me // 2
+    side = me % 2
+    buddy = me + 1 - 2 * side
+    base = 2 * half
+    far_base = 2 - base
+    far = 2 - half
+    inner = (me == 1) | (me == 2)
+    outer = (me == 0) | (me == 3)
+    chip_hops = sorted(range(1, chips), key=lambda s: (abs(2 * s - chips), s))
+    gg_hops = (2, 1, 3)
+
+    barrier = pltpu.get_barrier_semaphore()
+    for s in gg_hops:
+        pl.semaphore_signal(barrier, inc=1, device_id={"expert": (me + s) % experts})
+    for s in chip_hops:
+        pl.semaphore_signal(barrier, inc=1, device_id={"dp": (chip + s) % chips * 2 + core})
+    pl.semaphore_signal(barrier, inc=1, device_id={"dp": partner})
+
+    mine = pl.ds(pl.multiple_of(here * shard, shard), shard)
+    weights[0, mine, :] = wg_ref[...]
+    weights[1, mine, :] = wu_ref[...]
+    weights[2, mine, :] = wd_ref[...].T
+    pl.semaphore_wait(barrier, len(gg_hops) + len(chip_hops) + 1)
+
+    def copy(src, dst, send, recv, **to):
+        return pltpu.make_async_remote_copy(
+            src_ref=src, dst_ref=dst, send_sem=send, recv_sem=recv, device_id=to)
+
+    def shard_of(ref, owner):
+        return ref.at[:, pl.ds(pl.multiple_of(owner * shard, shard), shard), :]
+
+    def weight_send(target, sem):
+        return copy(shard_of(weights, here), shard_of(weights, here),
+                    ag_send.at[sem], ag_recv.at[here], dp=target)
+
+    def weight_forward(s):
+        source = (chip + s) % chips * 2 + core
+        return copy(shard_of(weights, source), shard_of(weights, source),
+                    fwd_send.at[s], ag_recv.at[source], dp=partner)
+
+    def weight_arrival(source):
+        return copy(shard_of(weights, here), shard_of(weights, source),
+                    ag_send.at[0], ag_recv.at[source], dp=partner)
+
+    def raw_copy(number):
+        return copy((tokens_ref, cot_ref)[number], (raw_x, raw_g)[number].at[side],
+                    raw_send.at[number], raw_recv.at[number, side], expert=far)
+
+    def raw_arrival(number, q):
+        return copy((tokens_ref, cot_ref)[number], (raw_x, raw_g)[number].at[q],
+                    raw_send.at[number], raw_recv.at[number, q], expert=far)
+
+    def meta_copy():
+        return copy(meta_ref, meta_in.at[side], meta_send, meta_recv.at[side], expert=far)
+
+    def meta_arrival(q):
+        return copy(meta_ref, meta_in.at[q], meta_send, meta_recv.at[q], expert=far)
+
+    def near_copy(number):
+        src = (x_buddy, g_buddy, y_out.at[buddy], e_out.at[buddy])[number]
+        dst = (x_in.at[me], g_in.at[me], y_near.at[side], e_near.at[side])[number]
+        return copy(src, dst, near_send.at[number], near_recv.at[number], expert=buddy)
+
+    def near_arrival(number):
+        src = (x_buddy, g_buddy, y_out.at[buddy], e_out.at[buddy])[number]
+        dst = (x_in.at[buddy], g_in.at[buddy], y_near.at[1 - side], e_near.at[1 - side])[number]
+        return copy(src, dst, near_send.at[number], near_recv.at[number], expert=buddy)
+
+    def fw_copy(number, q):
+        return copy((x_fw, g_fw)[number].at[q], (x_in, g_in)[number].at[far_base + q],
+                    fw_send.at[number, q], fw_recv.at[number, q], expert=buddy)
+
+    def far_copy(number, q):
+        return copy((y_out, e_out)[number].at[far_base + q], (y_far, e_far)[number].at[q, side],
+                    far_send.at[number, q], far_recv.at[number, q], expert=buddy)
+
+    def far_arrival(number, q):
+        return copy((y_out, e_out)[number].at[far_base + q],
+                    (y_far, e_far)[number].at[q, 1 - side],
+                    far_send.at[number, q], far_recv.at[number, q], expert=buddy)
+
+    def mix_copy(number, q):
+        return copy((y_part, e_part)[number].at[q], (y_mix, e_mix)[number],
+                    mix_send.at[number, q], mix_recv.at[number], expert=far_base + q)
+
+    def gg_copy(s):
+        target = (me + s) % experts
+        return copy(gg_out.at[target], gg_in.at[me], gg_send.at[s], gg_recv.at[me], expert=target)
+
+    def gg_arrival(s):
+        source = (me + s) % experts
+        return copy(gg_out.at[source], gg_in.at[source], gg_send.at[s], gg_recv.at[source],
+                    expert=source)
+
+    meta_copy().start()
+    raw_copy(0).start()
+    for s in chip_hops:
+        weight_send((chip + s) % chips * 2 + core, s).start()
+    weight_send(partner, 0).start()
+
+    earlier = jnp.where(
+        lax.broadcasted_iota(jnp.int32, (rows, rows), 0)
+        < lax.broadcasted_iota(jnp.int32, (rows, rows), 1), 1.0, 0.0).astype(BF16)
+    places = lax.broadcasted_iota(jnp.int32, (cap, rows), 0)
+
+    def picks_of(meta, e):
+        first = (meta[0:1].astype(jnp.int32) == e).astype(F32)
+        second = (meta[1:2].astype(jnp.int32) == e).astype(F32)
+        member = jnp.broadcast_to(first + second, (8, rows))
+        rank = dot(member.astype(BF16), earlier, ((1,), (0,)))
+        hit = (rank[0:1].astype(jnp.int32) == places).astype(F32)
+        return hit * first, hit * second
+
+    def gate_rows(meta, one, two):
+        return jnp.sum(one * meta[2:3] + two * meta[3:4], axis=1, keepdims=True)
+
+    meta = meta_ref[...]
+    for e in range(experts):
+        one, two = picks_of(meta, e)
+        pick_ref[e * cap:(e + 1) * cap, 0:rows] = one.astype(BF16)
+        pick_ref[e * cap:(e + 1) * cap, rows:2 * rows] = two.astype(BF16)
+
+    def home_picks(e):
+        at = pl.ds(pl.multiple_of(e * cap, cap), cap)
+        return pick_ref[at, 0:rows].astype(F32), pick_ref[at, rows:2 * rows].astype(F32)
+
+    one, two = home_picks(buddy)
+    place = (one + two).astype(BF16)
+    x_buddy[...] = dot(place, tokens_ref[...], ((1,), (0,))).astype(BF16)
+    near_copy(0).start()
+    raw_copy(1).start()
+    g_buddy[...] = (
+        gate_rows(meta, one, two) * dot(place, cot_ref[...], ((1,), (0,)))).astype(BF16)
+    near_copy(1).start()
+    one, two = home_picks(me)
+    place = (one + two).astype(BF16)
+    x_in[me] = dot(place, tokens_ref[...], ((1,), (0,))).astype(BF16)
+    g_in[me] = (
+        gate_rows(meta, one, two) * dot(place, cot_ref[...], ((1,), (0,)))).astype(BF16)
+
+    def forward_weights(s):
+        weight_arrival((chip + s) % chips * 2 + core).wait_recv()
+        weight_forward(s).start()
+
+    def relay_x(q):
+        meta_arrival(q).wait_recv()
+        theirs = meta_in[q]
+        at_buddy = pl.ds(pl.multiple_of((1 - side) * cap, cap), cap)
+        at_mine = pl.ds(pl.multiple_of(side * cap, cap), cap)
+        raw_arrival(0, q).wait_recv()
+        one, two = picks_of(theirs, buddy)
+        relay_pick[q, at_buddy, 0:rows] = one.astype(BF16)
+        relay_pick[q, at_buddy, rows:2 * rows] = two.astype(BF16)
+        x_fw[q] = dot((one + two).astype(BF16), raw_x[q], ((1,), (0,))).astype(BF16)
+        fw_copy(0, q).start()
+        one, two = picks_of(theirs, me)
+        relay_pick[q, at_mine, 0:rows] = one.astype(BF16)
+        relay_pick[q, at_mine, rows:2 * rows] = two.astype(BF16)
+        x_in[far_base + q] = dot((one + two).astype(BF16), raw_x[q], ((1,), (0,))).astype(BF16)
+
+    def relay_g(q):
+        theirs = meta_in[q]
+        raw_arrival(1, q).wait_recv()
+        for l, own in ((1 - side, False), (side, True)):
+            at = pl.ds(pl.multiple_of(l * cap, cap), cap)
+            one = relay_pick[q, at, 0:rows].astype(F32)
+            two = relay_pick[q, at, rows:2 * rows].astype(F32)
+            packed = (gate_rows(theirs, one, two)
+                      * dot((one + two).astype(BF16), raw_g[q], ((1,), (0,)))).astype(BF16)
+            if own:
+                g_in[far_base + q] = packed
+            else:
+                g_fw[q] = packed
+                fw_copy(1, q).start()
+
+    piece = 256
+
+    def relay_back(number, q):
+        far_arrival(number, q).wait_recv()
+        blocks = (y_far, e_far)[number]
+        blocks[q, side] = (y_out, e_out)[number][far_base + q]
+        eye = (lax.broadcasted_iota(jnp.int32, (rows, rows), 0)
+               == lax.broadcasted_iota(jnp.int32, (rows, rows), 1)).astype(F32)
+        gate_one = jnp.sum(eye * meta_in[q, 2:3], axis=1, keepdims=True)
+        gate_two = jnp.sum(eye * meta_in[q, 3:4], axis=1, keepdims=True)
+
+        @pl.loop(0, width // piece)
+        def _(i):
+            at = pl.ds(pl.multiple_of(i * piece, piece), piece)
+            y = blocks[q, :, :, at].reshape(2 * cap, piece)
+            per_entry = dot(relay_pick[q], y, ((0,), (0,)))
+            head, tail = per_entry[:rows], per_entry[rows:]
+            if number == 0:
+                head, tail = gate_one * head, gate_two * tail
+            (y_part, e_part)[number][q, :, at] = (head + tail).astype(BF16)
+
+        mix_copy(number, q).start()
+
+    forward_weights(chip_hops[-1])
+
+    @pl.when(inner)
+    def _():
+        relay_x(0)
+
+    for s in chip_hops[:-1]:
+        forward_weights(s)
+
+    @pl.when(inner)
+    def _():
+        relay_x(1)
+
+    weight_arrival(partner).wait_recv()
+    for s in reversed(chip_hops):
+        weight_arrival((chip + s) % chips * 2 + 1 - core).wait_recv()
+    near_arrival(0).wait_recv()
+
+    @pl.when(outer)
+    def _():
+        for q in range(2):
+            fw_copy(0, q).wait_recv()
+
+    steps = 2
+    per = experts // steps
+    tall = per * cap
+
+    @pl.loop(0, steps)
+    def _(i):
+        at = pl.ds(pl.multiple_of(i * tall, tall), tall)
+        x = x_in[pl.ds(i * per, per)].reshape(tall, width)
+        gate_pre = dot(x, weights[0], ((1,), (0,)))
+        up_pre = dot(x, weights[1], ((1,), (0,)))
+        gate_pre_ref[at, :] = gate_pre
+        up_pre_ref[at, :] = up_pre
+        hidden = (gate_pre * jax.nn.sigmoid(gate_pre) * up_pre).astype(BF16)
+        hidden_ref[at, :] = hidden
+        y_out[pl.ds(i * per, per)] = dot(hidden, weights[2], ((1,), (1,))).astype(BF16).reshape(
+            per, cap, width)
+
+    @pl.when(outer)
+    def _():
+        for q in range(2):
+            far_copy(0, q).start()
+
+    near_copy(2).start()
+    y_near[side] = y_out[me]
+
+    @pl.when(inner)
+    def _():
+        relay_g(0)
+        relay_g(1)
+        relay_back(0, 0)
+        relay_back(0, 1)
+
+    near_arrival(1).wait_recv()
+
+    @pl.when(outer)
+    def _():
+        for q in range(2):
+            fw_copy(1, q).wait_recv()
+
+    ones = jnp.ones((8, hidden_ref.shape[1]), BF16)
+
+    @pl.loop(0, steps)
+    def _(i):
+        at = pl.ds(pl.multiple_of(i * tall, tall), tall)
+        g = g_in[pl.ds(i * per, per)].reshape(tall, width)
+        d_hidden = dot(g, weights[2], ((1,), (0,)))
+        gate_pre = gate_pre_ref[at, :]
+        up_pre = up_pre_ref[at, :]
+        sigma = jax.nn.sigmoid(gate_pre)
+        d_gate = (d_hidden * up_pre * sigma * (1.0 + gate_pre * (1.0 - sigma))).astype(BF16)
+        d_up = (d_hidden * (gate_pre * sigma)).astype(BF16)
+        d_gate_ref[at, :] = d_gate
+        d_up_ref[at, :] = d_up
+        entry = dot(d_gate, weights[0], ((1,), (1,))) + dot(d_up, weights[1], ((1,), (1,)))
+        e_out[pl.ds(i * per, per)] = entry.astype(BF16).reshape(per, cap, width)
+        product = hidden_ref[at, :].astype(F32) * d_hidden
+        high = product.astype(BF16)
+        low = (product - high.astype(F32)).astype(BF16)
+        for j in range(per):
+            cut = slice(j * cap, (j + 1) * cap)
+            gg_out[i * per + j, :, 0:cap] = (
+                dot(ones, high[cut], ((1,), (1,))) + dot(ones, low[cut], ((1,), (1,))))
+
+    @pl.when(outer)
+    def _():
+        for q in range(2):
+            far_copy(1, q).start()
+
+    near_copy(3).start()
+    for s in gg_hops:
+        gg_copy(s).start()
+    e_near[side] = e_out[me]
+    gg_in[me] = gg_out[me]
+
+    @pl.loop(0, width // piece)
+    def _(i):
+        at = pl.ds(pl.multiple_of(i * piece, piece), piece)
+        x = x_in[:, :, at].reshape(slots, piece)
+        part[0, at, :] = dot(x, d_gate_ref[...], ((0,), (0,))).astype(BF16)
+        part[1, at, :] = dot(x, d_up_ref[...], ((0,), (0,))).astype(BF16)
+        g = g_in[:, :, at].reshape(slots, piece)
+        part[2, at, :] = dot(g, hidden_ref[...], ((0,), (0,))).astype(BF16)
+
+    def pair_send_of(s):
+        target = (chip + s) % chips
+        return copy(shard_of(part, target * 2 + 1 - core), pair_in.at[s],
+                    pair_send.at[s], pair_recv.at[s], dp=partner)
+
+    def share_send_of(s):
+        return copy(summed.at[s], rs_in.at[s], rs_send.at[s], rs_recv.at[s],
+                    dp=(chip + s) % chips * 2 + core)
+
+    def own_sum(s):
+        owner = (chip + s) % chips * 2 + core
+        own = part[:, pl.ds(pl.multiple_of(owner * shard, shard), shard), :]
+        return own.astype(F32) + pair_in[s].astype(F32)
+
+    for s in chip_hops + [0]:
+        pair_send_of(s).start()
+    for s in chip_hops:
+        pair_send_of(s).wait_recv()
+        summed[s] = own_sum(s).astype(BF16)
+        share_send_of(s).start()
+
+    @pl.when(inner)
+    def _():
+        relay_back(1, 0)
+        relay_back(1, 1)
+
+    for s in gg_hops:
+        gg_arrival(s).wait_recv()
+    sums = jnp.zeros((8, 2 * rows), F32)
+    for e in range(experts):
+        row = gg_in[e, :, 0:cap]
+        high = row.astype(BF16)
+        low = (row - high.astype(F32)).astype(BF16)
+        chosen = pick_ref[e * cap:(e + 1) * cap, :]
+        sums += dot(high, chosen, ((1,), (0,))) + dot(low, chosen, ((1,), (0,)))
+    gate_grads_ref[0:1, :] = sums[0:1, 0:rows] / meta_ref[2:3, :]
+    gate_grads_ref[1:2, :] = sums[0:1, rows:2 * rows] / meta_ref[3:4, :]
+
+    near_at = pl.ds(pl.multiple_of(half * (2 * cap), 2 * cap), 2 * cap)
+    near_arrival(2).wait_recv()
+    mix_copy(0, 0).wait_recv()
+
+    @pl.loop(0, width // piece)
+    def _(i):
+        at = pl.ds(pl.multiple_of(i * piece, piece), piece)
+        y = y_near[:, :, at].reshape(2 * cap, piece)
+        per_entry = dot(pick_ref[near_at, :], y, ((0,), (0,)))
+        mixed_ref[:, at] = (
+            gates_ref[:, 0:1] * per_entry[:rows] + gates_ref[:, 1:2] * per_entry[rows:]
+            + y_mix[:, at].astype(F32)).astype(BF16)
+
+    pair_send_of(0).wait_recv()
+    total = own_sum(0)
+    for s in reversed(chip_hops):
+        share_send_of(s).wait_recv()
+        total += rs_in[s].astype(F32)
+    share_g_ref[...] = total[0]
+    share_u_ref[...] = total[1]
+    share_d_ref[...] = total[2].T
+
+    near_arrival(3).wait_recv()
+    mix_copy(1, 0).wait_recv()
+
+    @pl.loop(0, width // piece)
+    def _(i):
+        at = pl.ds(pl.multiple_of(i * piece, piece), piece)
+        y = e_near[:, :, at].reshape(2 * cap, piece)
+        per_entry = dot(pick_ref[near_at, :], y, ((0,), (0,)))
+        token_grads_ref[:, at] = (
+            per_entry[:rows] + per_entry[rows:] + e_mix[:, at].astype(F32)).astype(BF16)
+
+    meta_copy().wait_send()
+    for number in range(2):
+        raw_copy(number).wait_send()
+    for number in range(4):
+        near_copy(number).wait_send()
+    for s in gg_hops:
+        gg_copy(s).wait_send()
+    for s in chip_hops:
+        weight_send((chip + s) % chips * 2 + core, s).wait_send()
+        weight_forward(s).wait_send()
+        pair_send_of(s).wait_send()
+        share_send_of(s).wait_send()
+    weight_send(partner, 0).wait_send()
+    pair_send_of(0).wait_send()
+
+    @pl.when(inner)
+    def _():
+        for number in range(2):
+            for q in range(2):
+                fw_copy(number, q).wait_send()
+                mix_copy(number, q).wait_send()
+
+    @pl.when(outer)
+    def _():
+        for number in range(2):
+            for q in range(2):
+                far_copy(number, q).wait_send()
+
+
+def relay_body(tokens, routes, gates, cotangent, w_gate, w_up, w_down):
+    experts = lax.axis_size("expert")
+    groups = lax.axis_size("dp")
+    rows, width = tokens.shape
+    picks = routes.shape[1]
+    hidden = w_gate.shape[2]
+    shard = w_gate.shape[1]
+    cap = max(2, 5 * rows * picks // (4 * experts))
+    cap = -(-cap // 16) * 16
+    lanes = -(-cap // 128) * 128
+    slots = experts * cap
+    chips = groups // 2
+    meta = jnp.concatenate(
+        [routes.T.astype(F32), gates.T, jnp.zeros((8 - 2 * picks, rows), F32)], axis=0)
+    vmem = pl.BlockSpec(memory_space=pltpu.VMEM)
+    dma = pltpu.SemaphoreType.DMA
+    blocks = lambda *lead: pltpu.VMEM((*lead, cap, width), BF16)
+    whole = lambda *lead: pltpu.VMEM((*lead, rows, width), BF16)
+    mixed, token_grads, gate_grads, share_g, share_u, share_d = pl.pallas_call(
+        functools.partial(relay_kernel, cap),
+        out_shape=(
+            jax.ShapeDtypeStruct((rows, width), BF16),
+            jax.ShapeDtypeStruct((rows, width), BF16),
+            jax.ShapeDtypeStruct((picks, rows), F32),
+            jax.ShapeDtypeStruct((shard, hidden), F32),
+            jax.ShapeDtypeStruct((shard, hidden), F32),
+            jax.ShapeDtypeStruct((hidden, shard), F32),
+        ),
+        in_specs=[vmem] * 7,
+        out_specs=(vmem,) * 6,
+        scratch_shapes=[
+            pltpu.VMEM((slots, picks * rows), BF16),
+            pltpu.VMEM((2, 2 * cap, picks * rows), BF16),
+            pltpu.VMEM((2, 8, rows), F32),
+            whole(2), whole(2),
+            blocks(), blocks(), blocks(2), blocks(2),
+            blocks(experts), blocks(experts), blocks(experts), blocks(experts),
+            blocks(2), blocks(2), blocks(2, 2), blocks(2, 2),
+            whole(2), whole(2), whole(), whole(),
+            pltpu.VMEM((experts, 8, lanes), F32), pltpu.VMEM((experts, 8, lanes), F32),
+            pltpu.VMEM((3, width, hidden), BF16),
+            pltpu.VMEM((slots, hidden), F32),
+            pltpu.VMEM((slots, hidden), F32),
+            pltpu.VMEM((slots, hidden), BF16),
+            pltpu.VMEM((slots, hidden), BF16),
+            pltpu.VMEM((slots, hidden), BF16),
+            pltpu.VMEM((3, width, hidden), BF16),
+            pltpu.VMEM((chips, 3, shard, hidden), BF16),
+            pltpu.VMEM((chips, 3, shard, hidden), BF16),
+            pltpu.VMEM((chips, 3, shard, hidden), BF16),
+            dma((2,)), dma((2, 2)), dma(()), dma((2,)), dma((4,)), dma((4,)),
+            dma((2, 2)), dma((2, 2)), dma((2, 2)), dma((2, 2)), dma((2, 2)), dma((2,)),
+            dma((experts,)), dma((experts,)),
+            dma((chips,)), dma((chips,)), dma((groups,)),
+            dma((chips,)), dma((chips,)), dma((chips,)), dma((chips,)),
+        ],
+        compiler_params=pltpu.CompilerParams(
+            collective_id=0, has_side_effects=True, vmem_limit_bytes=58 * 1024 * 1024
+        ),
+        name="routed_experts",
+    )(tokens, cotangent, gates, meta, w_gate[0], w_up[0], w_down[0])
+    return (mixed, token_grads, gate_grads.T, share_g[None], share_u[None], share_d[None])
+
+
+def body(*arguments):
+    relayed = lax.axis_size("expert") == 4 and arguments[4].shape[1] % 128 == 0
+    return (relay_body if relayed else direct_body)(*arguments)
+
+
 def solution(mesh):
     return jax.shard_map(
         body,

time: 147 us -> 151 us (1.027)
  the two profiles are of different devices: /device:TPU:13 before, /device:TPU:5 now
where the time goes in v2:
time: 151 us
  Pallas kernels  141 us (93%)
  local copies, waits for them, and re-layouts  8.42 us (6%)
    pallas_call x1, Pallas kernels, relay_body(): pl.pallas_call(functools.partial(relay_kernel, cap), out_shape=(jax.Shape...  141 us
    unnamed x21, local copies, waits for them, and re-layouts  8.34 us

profile of v2, /device:TPU:5, one launch (start us, length us, event | category | flops | bytes accessed | tf_op | source)
XLA Modules:
  0.0 151.1 jit_solution(17904986186652106963)
XLA Ops:
  0.6 0.0 copy-start.5
  0.7 0.1 pad.2.clone
  0.7 0.6 copy-done.5
  1.3 0.0 copy-start.4
  1.3 0.7 copy-done.4
  2.0 0.7 maximum_maximum_fusion.meta_ref
  2.7 0.7 copy.13.gates_ref
  3.4 141.4 %routed_experts.1 = (bf16[128,2048]{1,0:T(8,128)(2,1)}, bf16[128,2048]{1,0:T(8,128)(2,1)}, f32[2,128]{1,0:T(2,128)}, f32[256,384]{1,0:T(8,128)}, f32[256,384]{1,0:T(8,128)}, /*index=5*/f32[384,256]{1,0:T(8,128)}) custom-call(bf16[128,2048]{1,0:T(8,128)(2,1)} %tokens_ref.1, bf16[128,2048]{1,0:T(8,128)(2,1)} %cot_ref.1, f32[128,2]{1,0:T(8,128)} %copy.13.gates_ref, ...), custom_call_target="tpu_custom_call" | custom-call | tf_op jit(solution)/shard_map/routed_experts/pallas_call | solution.py:766
  144.8 0.0 copy-start
  144.8 1.9 %copy.20 = bf16[128,2048]{1,0:T(8,128)(2,1)} copy(bf16[128,2048]{1,0:T(8,128)(2,1)} %get-tuple-element.24) | data formatting | bytes 1048576
  146.7 0.0 copy-done
  146.7 0.0 copy-start.6
  146.7 0.0 copy-start.3
  146.7 0.8 copy.21
  147.5 0.0 copy-done.6
  147.5 0.6 copy.22
  148.1 0.0 copy-done.3
  148.1 0.0 copy-start.2
  148.1 0.7 copy.23
  148.9 0.4 copy-done.2
  149.2 0.0 copy-start.1
  149.2 0.7 copy.24
  150.0 0.4 copy-done.1
  150.4 0.7 copy.25
  (2 shorter events, 0.0 us)
Async XLA Ops:
  0.6 0.7 copy-start.5
  1.3 0.7 copy-start.4
  144.8 2.0 %copy-start = (bf16[128,2048]{1,0:T(8,128)(2,1)S(1)}, bf16[128,2048]{1,0:T(8,128)(2,1)}, u32[]{:S(2)}) copy-start(bf16[128,2048]{1,0:T(8,128)(2,1)} %get-tuple-element.25) | copy-start | bytes 1572868
  146.7 0.8 copy-start.6
  146.7 1.4 copy-start.3
  148.1 1.1 copy-start.2
  149.2 1.1 copy-start.1

commit v3 on v2

--- a/solution.py
+++ b/solution.py
@@ -318,16 +318,15 @@
     return (mixed, token_grads, gate_grads, share[0][None], share[1][None], share[2].T[None])
 
 
-def relay_kernel(
+def line_kernel(
     cap,
     tokens_ref, cot_ref, gates_ref, meta_ref, wg_ref, wu_ref, wd_ref,
     mixed_ref, token_grads_ref, gate_grads_ref, share_g_ref, share_u_ref, share_d_ref,
-    pick_ref, relay_pick, meta_in, raw_x, raw_g, x_buddy, g_buddy, x_fw, g_fw, x_in, g_in,
-    y_out, e_out, y_near, e_near, y_far, e_far, y_part, e_part, y_mix, e_mix, gg_out, gg_in,
+    pick_ref, x_out, g_out, x_in, g_in,
+    y_out, e_out, y_in, e_in, gg_out, gg_in,
     weights, gate_pre_ref, up_pre_ref, hidden_ref, d_gate_ref, d_up_ref,
     part, pair_in, summed, rs_in,
-    raw_send, raw_recv, meta_send, meta_recv, near_send, near_recv, fw_send, fw_recv,
-    far_send, far_recv, mix_send, mix_recv, gg_send, gg_recv,
+    back_send, back_recv, gg_send, gg_recv,
     ag_send, fwd_send, ag_recv, pair_send, pair_recv, rs_send, rs_recv,
 ):
     experts = 4
@@ -344,11 +343,7 @@
     half = me // 2
     side = me % 2
     buddy = me + 1 - 2 * side
-    base = 2 * half
-    far_base = 2 - base
-    far = 2 - half
-    inner = (me == 1) | (me == 2)
-    outer = (me == 0) | (me == 3)
+    far_base = 2 - 2 * half
     chip_hops = sorted(range(1, chips), key=lambda s: (abs(2 * s - chips), s))
     gg_hops = (2, 1, 3)
 
@@ -385,46 +380,17 @@
         return copy(shard_of(weights, here), shard_of(weights, source),
                     ag_send.at[0], ag_recv.at[source], dp=partner)
 
-    def raw_copy(number):
-        return copy((tokens_ref, cot_ref)[number], (raw_x, raw_g)[number].at[side],
-                    raw_send.at[number], raw_recv.at[number, side], expert=far)
-
-    def raw_arrival(number, q):
-        return copy((tokens_ref, cot_ref)[number], (raw_x, raw_g)[number].at[q],
-                    raw_send.at[number], raw_recv.at[number, q], expert=far)
-
-    def meta_copy():
-        return copy(meta_ref, meta_in.at[side], meta_send, meta_recv.at[side], expert=far)
-
-    def meta_arrival(q):
-        return copy(meta_ref, meta_in.at[q], meta_send, meta_recv.at[q], expert=far)
-
-    def near_copy(number):
-        src = (x_buddy, g_buddy, y_out.at[buddy], e_out.at[buddy])[number]
-        dst = (x_in.at[me], g_in.at[me], y_near.at[side], e_near.at[side])[number]
-        return copy(src, dst, near_send.at[number], near_recv.at[number], expert=buddy)
-
-    def near_arrival(number):
-        src = (x_buddy, g_buddy, y_out.at[buddy], e_out.at[buddy])[number]
-        dst = (x_in.at[buddy], g_in.at[buddy], y_near.at[1 - side], e_near.at[1 - side])[number]
-        return copy(src, dst, near_send.at[number], near_recv.at[number], expert=buddy)
-
-    def fw_copy(number, q):
-        return copy((x_fw, g_fw)[number].at[q], (x_in, g_in)[number].at[far_base + q],
-                    fw_send.at[number, q], fw_recv.at[number, q], expert=buddy)
-
-    def far_copy(number, q):
-        return copy((y_out, e_out)[number].at[far_base + q], (y_far, e_far)[number].at[q, side],
-                    far_send.at[number, q], far_recv.at[number, q], expert=buddy)
-
-    def far_arrival(number, q):
-        return copy((y_out, e_out)[number].at[far_base + q],
-                    (y_far, e_far)[number].at[q, 1 - side],
-                    far_send.at[number, q], far_recv.at[number, q], expert=buddy)
-
-    def mix_copy(number, q):
-        return copy((y_part, e_part)[number].at[q], (y_mix, e_mix)[number],
-                    mix_send.at[number, q], mix_recv.at[number], expert=far_base + q)
+    others = (far_base + side, far_base + 1 - side, buddy)
+
+    def back_copy(number, i):
+        return copy((x_out, g_out, y_out, e_out)[number].at[others[i]],
+                    (x_in, g_in, y_in, e_in)[number].at[me],
+                    back_send.at[number, i], back_recv.at[number, me], expert=others[i])
+
+    def back_arrival(number, i):
+        return copy((x_out, g_out, y_out, e_out)[number].at[others[i]],
+                    (x_in, g_in, y_in, e_in)[number].at[others[i]],
+                    back_send.at[number, i], back_recv.at[number, others[i]], expert=others[i])
 
     def gg_copy(s):
         target = (me + s) % experts
@@ -435,8 +401,6 @@
         return copy(gg_out.at[source], gg_in.at[source], gg_send.at[s], gg_recv.at[source],
                     expert=source)
 
-    meta_copy().start()
-    raw_copy(0).start()
     for s in chip_hops:
         weight_send((chip + s) % chips * 2 + core, s).start()
     weight_send(partner, 0).start()
@@ -467,100 +431,36 @@
         at = pl.ds(pl.multiple_of(e * cap, cap), cap)
         return pick_ref[at, 0:rows].astype(F32), pick_ref[at, rows:2 * rows].astype(F32)
 
-    one, two = home_picks(buddy)
-    place = (one + two).astype(BF16)
-    x_buddy[...] = dot(place, tokens_ref[...], ((1,), (0,))).astype(BF16)
-    near_copy(0).start()
-    raw_copy(1).start()
-    g_buddy[...] = (
-        gate_rows(meta, one, two) * dot(place, cot_ref[...], ((1,), (0,)))).astype(BF16)
-    near_copy(1).start()
-    one, two = home_picks(me)
-    place = (one + two).astype(BF16)
-    x_in[me] = dot(place, tokens_ref[...], ((1,), (0,))).astype(BF16)
-    g_in[me] = (
-        gate_rows(meta, one, two) * dot(place, cot_ref[...], ((1,), (0,)))).astype(BF16)
+    for i, target in enumerate(others + (me,)):
+        one, two = home_picks(target)
+        x_out[target] = dot(
+            (one + two).astype(BF16), tokens_ref[...], ((1,), (0,))).astype(BF16)
+        if i < 3:
+            back_copy(0, i).start()
+        else:
+            x_in[me] = x_out[me]
+    for i, target in enumerate(others + (me,)):
+        one, two = home_picks(target)
+        g_out[target] = (gate_rows(meta, one, two) * dot(
+            (one + two).astype(BF16), cot_ref[...], ((1,), (0,)))).astype(BF16)
+        if i < 3:
+            back_copy(1, i).start()
+        else:
+            g_in[me] = g_out[me]
 
     def forward_weights(s):
         weight_arrival((chip + s) % chips * 2 + core).wait_recv()
         weight_forward(s).start()
 
-    def relay_x(q):
-        meta_arrival(q).wait_recv()
-        theirs = meta_in[q]
-        at_buddy = pl.ds(pl.multiple_of((1 - side) * cap, cap), cap)
-        at_mine = pl.ds(pl.multiple_of(side * cap, cap), cap)
-        raw_arrival(0, q).wait_recv()
-        one, two = picks_of(theirs, buddy)
-        relay_pick[q, at_buddy, 0:rows] = one.astype(BF16)
-        relay_pick[q, at_buddy, rows:2 * rows] = two.astype(BF16)
-        x_fw[q] = dot((one + two).astype(BF16), raw_x[q], ((1,), (0,))).astype(BF16)
-        fw_copy(0, q).start()
-        one, two = picks_of(theirs, me)
-        relay_pick[q, at_mine, 0:rows] = one.astype(BF16)
-        relay_pick[q, at_mine, rows:2 * rows] = two.astype(BF16)
-        x_in[far_base + q] = dot((one + two).astype(BF16), raw_x[q], ((1,), (0,))).astype(BF16)
-
-    def relay_g(q):
-        theirs = meta_in[q]
-        raw_arrival(1, q).wait_recv()
-        for l, own in ((1 - side, False), (side, True)):
-            at = pl.ds(pl.multiple_of(l * cap, cap), cap)
-            one = relay_pick[q, at, 0:rows].astype(F32)
-            two = relay_pick[q, at, rows:2 * rows].astype(F32)
-            packed = (gate_rows(theirs, one, two)
-                      * dot((one + two).astype(BF16), raw_g[q], ((1,), (0,)))).astype(BF16)
-            if own:
-                g_in[far_base + q] = packed
-            else:
-                g_fw[q] = packed
-                fw_copy(1, q).start()
-
     piece = 256
 
-    def relay_back(number, q):
-        far_arrival(number, q).wait_recv()
-        blocks = (y_far, e_far)[number]
-        blocks[q, side] = (y_out, e_out)[number][far_base + q]
-        eye = (lax.broadcasted_iota(jnp.int32, (rows, rows), 0)
-               == lax.broadcasted_iota(jnp.int32, (rows, rows), 1)).astype(F32)
-        gate_one = jnp.sum(eye * meta_in[q, 2:3], axis=1, keepdims=True)
-        gate_two = jnp.sum(eye * meta_in[q, 3:4], axis=1, keepdims=True)
-
-        @pl.loop(0, width // piece)
-        def _(i):
-            at = pl.ds(pl.multiple_of(i * piece, piece), piece)
-            y = blocks[q, :, :, at].reshape(2 * cap, piece)
-            per_entry = dot(relay_pick[q], y, ((0,), (0,)))
-            head, tail = per_entry[:rows], per_entry[rows:]
-            if number == 0:
-                head, tail = gate_one * head, gate_two * tail
-            (y_part, e_part)[number][q, :, at] = (head + tail).astype(BF16)
-
-        mix_copy(number, q).start()
-
-    forward_weights(chip_hops[-1])
-
-    @pl.when(inner)
-    def _():
-        relay_x(0)
-
-    for s in chip_hops[:-1]:
+    for s in reversed(chip_hops):
         forward_weights(s)
-
-    @pl.when(inner)
-    def _():
-        relay_x(1)
-
     weight_arrival(partner).wait_recv()
     for s in reversed(chip_hops):
         weight_arrival((chip + s) % chips * 2 + 1 - core).wait_recv()
-    near_arrival(0).wait_recv()
-
-    @pl.when(outer)
-    def _():
-        for q in range(2):
-            fw_copy(0, q).wait_recv()
+    for i in range(3):
+        back_arrival(0, i).wait_recv()
 
     steps = 2
     per = experts // steps
@@ -579,27 +479,12 @@
         y_out[pl.ds(i * per, per)] = dot(hidden, weights[2], ((1,), (1,))).astype(BF16).reshape(
             per, cap, width)
 
-    @pl.when(outer)
-    def _():
-        for q in range(2):
-            far_copy(0, q).start()
-
-    near_copy(2).start()
-    y_near[side] = y_out[me]
-
-    @pl.when(inner)
-    def _():
-        relay_g(0)
-        relay_g(1)
-        relay_back(0, 0)
-        relay_back(0, 1)
-
-    near_arrival(1).wait_recv()
-
-    @pl.when(outer)
-    def _():
-        for q in range(2):
-            fw_copy(1, q).wait_recv()
+    for i in range(3):
+        back_copy(2, i).start()
+    y_in[me] = y_out[me]
+
+    for i in range(3):
+        back_arrival(1, i).wait_recv()
 
     ones = jnp.ones((8, hidden_ref.shape[1]), BF16)
 
@@ -625,15 +510,11 @@
             gg_out[i * per + j, :, 0:cap] = (
                 dot(ones, high[cut], ((1,), (1,))) + dot(ones, low[cut], ((1,), (1,))))
 
-    @pl.when(outer)
-    def _():
-        for q in range(2):
-            far_copy(1, q).start()
-
-    near_copy(3).start()
     for s in gg_hops:
         gg_copy(s).start()
-    e_near[side] = e_out[me]
+    for i in range(3):
+        back_copy(3, i).start()
+    e_in[me] = e_out[me]
     gg_in[me] = gg_out[me]
 
     @pl.loop(0, width // piece)
@@ -665,11 +546,6 @@
         pair_send_of(s).wait_recv()
         summed[s] = own_sum(s).astype(BF16)
         share_send_of(s).start()
-
-    @pl.when(inner)
-    def _():
-        relay_back(1, 0)
-        relay_back(1, 1)
 
     for s in gg_hops:
         gg_arrival(s).wait_recv()
@@ -683,18 +559,17 @@
     gate_grads_ref[0:1, :] = sums[0:1, 0:rows] / meta_ref[2:3, :]
     gate_grads_ref[1:2, :] = sums[0:1, rows:2 * rows] / meta_ref[3:4, :]
 
-    near_at = pl.ds(pl.multiple_of(half * (2 * cap), 2 * cap), 2 * cap)
-    near_arrival(2).wait_recv()
-    mix_copy(0, 0).wait_recv()
+    for i in range(3):
+        back_arrival(2, i).wait_recv()
 
     @pl.loop(0, width // piece)
     def _(i):
         at = pl.ds(pl.multiple_of(i * piece, piece), piece)
-        y = y_near[:, :, at].reshape(2 * cap, piece)
-        per_entry = dot(pick_ref[near_at, :], y, ((0,), (0,)))
+        y = y_in[:, :, at].reshape(slots, piece)
+        per_entry = dot(pick_ref[...], y, ((0,), (0,)))
         mixed_ref[:, at] = (
             gates_ref[:, 0:1] * per_entry[:rows] + gates_ref[:, 1:2] * per_entry[rows:]
-            + y_mix[:, at].astype(F32)).astype(BF16)
+        ).astype(BF16)
 
     pair_send_of(0).wait_recv()
     total = own_sum(0)
@@ -705,22 +580,19 @@
     share_u_ref[...] = total[1]
     share_d_ref[...] = total[2].T
 
-    near_arrival(3).wait_recv()
-    mix_copy(1, 0).wait_recv()
+    either = pick_ref[:, 0:rows] + pick_ref[:, rows:2 * rows]
+    for i in range(3):
+        back_arrival(3, i).wait_recv()
 
     @pl.loop(0, width // piece)
     def _(i):
         at = pl.ds(pl.multiple_of(i * piece, piece), piece)
-        y = e_near[:, :, at].reshape(2 * cap, piece)
-        per_entry = dot(pick_ref[near_at, :], y, ((0,), (0,)))
-        token_grads_ref[:, at] = (
-            per_entry[:rows] + per_entry[rows:] + e_mix[:, at].astype(F32)).astype(BF16)
-
-    meta_copy().wait_send()
-    for number in range(2):
-        raw_copy(number).wait_send()
+        token_grads_ref[:, at] = dot(
+            either, e_in[:, :, at].reshape(slots, piece), ((0,), (0,))).astype(BF16)
+
     for number in range(4):
-        near_copy(number).wait_send()
+        for i in range(3):
+            back_copy(number, i).wait_send()
     for s in gg_hops:
         gg_copy(s).wait_send()
     for s in chip_hops:
@@ -731,21 +603,8 @@
     weight_send(partner, 0).wait_send()
     pair_send_of(0).wait_send()
 
-    @pl.when(inner)
-    def _():
-        for number in range(2):
-            for q in range(2):
-                fw_copy(number, q).wait_send()
-                mix_copy(number, q).wait_send()
-
-    @pl.when(outer)
-    def _():
-        for number in range(2):
-            for q in range(2):
-                far_copy(number, q).wait_send()
-
-
-def relay_body(tokens, routes, gates, cotangent, w_gate, w_up, w_down):
+
+def line_body(tokens, routes, gates, cotangent, w_gate, w_up, w_down):
     experts = lax.axis_size("expert")
     groups = lax.axis_size("dp")
     rows, width = tokens.shape
@@ -762,9 +621,8 @@
     vmem = pl.BlockSpec(memory_space=pltpu.VMEM)
     dma = pltpu.SemaphoreType.DMA
     blocks = lambda *lead: pltpu.VMEM((*lead, cap, width), BF16)
-    whole = lambda *lead: pltpu.VMEM((*lead, rows, width), BF16)
     mixed, token_grads, gate_grads, share_g, share_u, share_d = pl.pallas_call(
-        functools.partial(relay_kernel, cap),
+        functools.partial(line_kernel, cap),
         out_shape=(
             jax.ShapeDtypeStruct((rows, width), BF16),
             jax.ShapeDtypeStruct((rows, width), BF16),
@@ -777,13 +635,8 @@
         out_specs=(vmem,) * 6,
         scratch_shapes=[
             pltpu.VMEM((slots, picks * rows), BF16),
-            pltpu.VMEM((2, 2 * cap, picks * rows), BF16),
-            pltpu.VMEM((2, 8, rows), F32),
-            whole(2), whole(2),
-            blocks(), blocks(), blocks(2), blocks(2),
-            blocks(experts), blocks(experts), blocks(experts), blocks(experts),
-            blocks(2), blocks(2), blocks(2, 2), blocks(2, 2),
-            whole(2), whole(2), whole(), whole(),
+            blocks(experts), blocks(experts), blocks(experts), blocks(experts), blocks(experts), blocks(experts),
+            blocks(experts), blocks(experts),
             pltpu.VMEM((experts, 8, lanes), F32), pltpu.VMEM((experts, 8, lanes), F32),
             pltpu.VMEM((3, width, hidden), BF16),
             pltpu.VMEM((slots, hidden), F32),
@@ -795,8 +648,7 @@
             pltpu.VMEM((chips, 3, shard, hidden), BF16),
             pltpu.VMEM((chips, 3, shard, hidden), BF16),
             pltpu.VMEM((chips, 3, shard, hidden), BF16),
-            dma((2,)), dma((2, 2)), dma(()), dma((2,)), dma((4,)), dma((4,)),
-            dma((2, 2)), dma((2, 2)), dma((2, 2)), dma((2, 2)), dma((2, 2)), dma((2,)),
+            dma((4, 3)), dma((4, experts)),
             dma((experts,)), dma((experts,)),
             dma((chips,)), dma((chips,)), dma((groups,)),
             dma((chips,)), dma((chips,)), dma((chips,)), dma((chips,)),
@@ -810,8 +662,8 @@
 
 
 def body(*arguments):
-    relayed = lax.axis_size("expert") == 4 and arguments[4].shape[1] % 128 == 0
-    return (relay_body if relayed else direct_body)(*arguments)
+    in_line = lax.axis_size("expert") == 4 and arguments[4].shape[1] % 128 == 0
+    return (line_body if in_line else direct_body)(*arguments)
 
 
 def solution(mesh):

time: 151 us -> 142 us (0.940)
  the two profiles are of different devices: /device:TPU:5 before, /device:TPU:13 now
where the time goes in v3:
time: 142 us; the launch traced here: 141 us
  Pallas kernels  132 us (93%)
  local copies, waits for them, and re-layouts  8.42 us (6%)
    pallas_call x1, Pallas kernels, line_body(): pl.pallas_call(functools.partial(line_kernel, cap), out_shape=(jax.ShapeD...  132 us
    unnamed x21, local copies, waits for them, and re-layouts  8.34 us

profile of v3, /device:TPU:13, one launch (start us, length us, event | category | flops | bytes accessed | tf_op | source)
XLA Modules:
  0.0 141.3 jit_solution(12179321953509406660)
XLA Ops:
  0.6 0.0 copy-start.5
  0.7 0.1 pad.2.clone
  0.7 0.6 copy-done.5
  1.3 0.0 copy-start.4
  1.3 0.7 copy-done.4
  2.0 0.7 maximum_maximum_fusion.meta_ref
  2.7 0.7 copy.13.gates_ref
  3.4 131.5 %routed_experts.1 = (bf16[128,2048]{1,0:T(8,128)(2,1)}, bf16[128,2048]{1,0:T(8,128)(2,1)}, f32[2,128]{1,0:T(2,128)}, f32[256,384]{1,0:T(8,128)}, f32[256,384]{1,0:T(8,128)}, /*index=5*/f32[384,256]{1,0:T(8,128)}) custom-call(bf16[128,2048]{1,0:T(8,128)(2,1)} %tokens_ref.1, bf16[128,2048]{1,0:T(8,128)(2,1)} %cot_ref.1, f32[128,2]{1,0:T(8,128)} %copy.13.gates_ref, ...), custom_call_target="tpu_custom_call" | custom-call | tf_op jit(solution)/shard_map/routed_experts/pallas_call | solution.py:624
  134.9 0.0 copy-start
  134.9 1.9 %copy.20 = bf16[128,2048]{1,0:T(8,128)(2,1)} copy(bf16[128,2048]{1,0:T(8,128)(2,1)} %get-tuple-element.24) | data formatting | bytes 1048576
  136.9 0.0 copy-done
  136.9 0.0 copy-start.6
  136.9 0.0 copy-start.3
  136.9 0.8 copy.21
  137.7 0.0 copy-done.6
  137.7 0.6 copy.22
  138.2 0.0 copy-done.3
  138.2 0.0 copy-start.2
  138.2 0.7 copy.23
  139.0 0.4 copy-done.2
  139.4 0.0 copy-start.1
  139.4 0.7 copy.24
  140.1 0.4 copy-done.1
  140.5 0.7 copy.25
  (2 shorter events, 0.0 us)
Async XLA Ops:
  0.6 0.7 copy-start.5
  1.3 0.7 copy-start.4
  134.9 2.0 %copy-start = (bf16[128,2048]{1,0:T(8,128)(2,1)S(1)}, bf16[128,2048]{1,0:T(8,128)(2,1)}, u32[]{:S(2)}) copy-start(bf16[128,2048]{1,0:T(8,128)(2,1)} %get-tuple-element.25) | copy-start | bytes 1572868
  136.9 0.8 copy-start.6
  136.9 1.4 copy-start.3
  138.2 1.1 copy-start.2
  139.4 1.1 copy-start.1
